TPU v7x, 32 devices: a whole 2x2x4 slice. The times are simulated.
32 devices in a mesh: group: 4 (over z), expert: 8 (over y, x, core).
Axes of the slice: x: 2, y: 2, z: 4, core: 2. Of those that a mesh axis runs over, the one named last changes fastest.
Arguments:
- group_logits: float32 [4096, 4], P(('group', 'expert')), may hold values from -6 to 6
- expert_logits: float32 [4096, 32], P(('group', 'expert')), may hold values from -6 to 6
- expert_ids: int32 [4096, 2], P(('group', 'expert')), may hold values from 0 to 31, all different within a row; in each aligned block of 128 rows (0 to 127, 128 to 255, ...) at most 16 rows name the same one
- cotangent: bfloat16 [4096, 3584], P(('group', 'expert')), may hold values from -6 to 6
- hidden_saved: bfloat16 [32, 512, 1024], P(('group', 'expert')), may hold values from -0.1875 to 0.1875
- w_down: bfloat16 [32, 1024, 3584], P(('group', 'expert')), may hold values from -0.1875 to 0.1875
Outputs:
- hidden_grad: bfloat16 [32, 512, 1024], P(('group', 'expert'))
- d_group_logits: float32 [4096, 4], P(('group', 'expert'))
- d_expert_logits: float32 [4096, 32], P(('group', 'expert'))
Inputs may be any that keep to these rules, and one draw needn't show every extreme that they name: `expert_ids`: within the 128 tokens of one device no expert is named by more than 16 choices, a bound that some block reaches; the 2 experts of a token differ.
All inputs are finite; a program needn't handle non-finite values.
Results may differ from a plain program's by a relative error of at most 0.0045.
Values may be sent and summed in bfloat16 or wider, within the bound.
No kernel may reach another device: no remote copies, remote signals or barrier semaphores. Data moves between devices by JAX's collectives and lax.ppermute only.
A program may use at most 64 MiB of HBM per device.

v0:
```python
from functools import partial
import jax
import jax.numpy as jnp
from jax import lax
from jax.sharding import PartitionSpec as P

ITERS = 5
SOFTCAP = 4.0


def capped(logits):
    return jnp.exp(SOFTCAP * jnp.tanh(logits / SOFTCAP))


def squashing(logits):
    bounded = jnp.tanh(logits / SOFTCAP)
    return 1.0 - bounded * bounded


def balance_level(level_in, target, column_sum):
    scaled = level_in * (target / column_sum)
    return (scaled, jnp.sum(scaled, -1, keepdims=True))


def adjoint_local(out_grad, level_in, target, column_sum):
    scaled, row_total = balance_level(level_in, target, column_sum)
    level_out = scaled / row_total
    scaled_grad = (out_grad - jnp.sum(out_grad * level_out, -1, keepdims=True)) / row_total
    return (scaled_grad, jnp.sum(scaled_grad * level_in, 0))


def adjoint_finish(scaled_grad, inner, target, column_sum):
    return target / column_sum * (scaled_grad - inner / column_sum)


def balance_step(targets, current, unused):
    target_group, target_expert = targets
    group_in, expert_in = current
    group_cols, expert_cols = lax.psum(
        (jnp.sum(group_in, 0), jnp.sum(expert_in, 0)), ("group", "expert")
    )
    scaled_g, rowsum_g = balance_level(group_in, target_group, group_cols)
    scaled_e, rowsum_e = balance_level(expert_in, target_expert, expert_cols)
    return (
        (scaled_g / rowsum_g, scaled_e / rowsum_e),
        (group_in, expert_in, group_cols, expert_cols),
    )


def adjoint_step(targets, carried, stored_step):
    target_group, target_expert = targets
    grad_g, grad_e = carried
    group_in, expert_in, group_cols, expert_cols = stored_step
    scaled_g, inner_g = adjoint_local(grad_g, group_in, target_group, group_cols)
    scaled_e, inner_e = adjoint_local(grad_e, expert_in, target_expert, expert_cols)
    inner_g, inner_e = lax.psum((inner_g, inner_e), ("group", "expert"))
    next_g = adjoint_finish(scaled_g, inner_g, target_group, group_cols)
    next_e = adjoint_finish(scaled_e, inner_e, target_expert, expert_cols)
    return ((next_g, next_e), None)


def deliver(payload):
    halfway = (
        lax.all_to_all(payload[0], "expert", split_axis=1, concat_axis=1, tiled=True),
        lax.all_to_all(payload[1], "expert", split_axis=1, concat_axis=1, tiled=True),
    )
    return (
        lax.all_to_all(halfway[0], "group", split_axis=0, concat_axis=0, tiled=True),
        lax.all_to_all(halfway[1], "group", split_axis=0, concat_axis=0, tiled=True),
    )


def per_device(group_logits, expert_logits, expert_ids, cotangent, hidden_saved, w_down):
    groups = lax.axis_size("group")
    per_group = lax.axis_size("expert")
    experts = groups * per_group
    tokens_here = cotangent.shape[0]
    top_count = expert_ids.shape[1]
    model_width = cotangent.shape[1]
    capacity = hidden_saved.shape[1] // experts
    targets = (float(tokens_here * per_group), float(tokens_here * groups))
    flat_ids = expert_ids.reshape(-1)
    picked = (flat_ids[:, None] == jnp.arange(experts, dtype=jnp.int32)[None, :]).astype(jnp.int32)
    positions = jnp.sum((jnp.cumsum(picked, 0) - picked) * picked, 1)
    slot_index = flat_ids * capacity + positions
    serial = jnp.arange(flat_ids.shape[0], dtype=jnp.int32)
    source_index = jnp.zeros((experts * capacity,), jnp.int32).at[slot_index].set(serial)
    filled = jnp.zeros((experts * capacity,), jnp.int32).at[slot_index].set(1)
    fetched = jnp.take(cotangent, source_index // top_count, axis=0)
    send_rows = jnp.where(filled[:, None] > 0, fetched, jnp.zeros_like(fetched))
    send_rows = send_rows.reshape(groups, per_group, capacity, model_width)
    group_of = expert_ids // per_group
    group_aff = capped(group_logits)
    expert_aff = capped(expert_logits).reshape(tokens_here, groups, per_group)
    (group_prob, expert_prob), stored = lax.scan(
        partial(balance_step, targets), (group_aff, expert_aff), None, length=ITERS
    )
    pick_group = jnp.take_along_axis(group_prob, group_of, 1)
    pick_expert = jnp.take_along_axis(expert_prob.reshape(tokens_here, experts), expert_ids, 1)
    pair_prob = pick_group * pick_expert
    total_prob = jnp.sum(pair_prob, 1, keepdims=True)
    gate_prob = pair_prob / total_prob
    gate_sent = (
        jnp.zeros((experts * capacity,), jnp.bfloat16)
        .at[slot_index]
        .set(gate_prob.astype(jnp.bfloat16).reshape(-1))
    )
    gate_sent = gate_sent.reshape(groups, per_group, capacity)
    routed = (
        group_aff,
        expert_aff,
        stored,
        pick_group,
        pick_expert,
        total_prob,
        gate_prob,
        gate_sent,
    )
    got_rows, got_gates = deliver((send_rows, routed[7]))
    group_aff, expert_aff, stored, pick_group, pick_expert, total_prob, gate_prob, unused_gates = (
        routed
    )
    weight = w_down[0]
    saved_hidden = hidden_saved[0]
    expert_rows = got_rows.reshape(-1, model_width)
    unscaled = lax.dot_general(
        expert_rows, weight, (((1,), (1,)), ((), ())), preferred_element_type=jnp.float32
    )
    slot_grad = jnp.sum(unscaled * saved_hidden.astype(jnp.float32), 1)
    grad_rows = (got_gates.reshape(-1, 1).astype(jnp.float32) * unscaled).astype(jnp.bfloat16)
    hidden_grad = grad_rows[None]
    answers = lax.all_to_all(
        lax.all_to_all(
            slot_grad.reshape(groups, per_group, capacity),
            "group",
            split_axis=0,
            concat_axis=0,
            tiled=True,
        ),
        "expert",
        split_axis=1,
        concat_axis=1,
        tiled=True,
    )
    gate_grad = answers.reshape(-1)[slot_index].reshape(tokens_here, top_count)
    pair_grad = (gate_grad - jnp.sum(gate_prob * gate_grad, 1, keepdims=True)) / total_prob
    group_pick = (
        group_of[:, :, None] == jnp.arange(groups, dtype=jnp.int32)[None, None, :]
    ).astype(jnp.float32)
    seed_group = jnp.sum(group_pick * (pair_grad * pick_expert)[:, :, None], 1)
    expert_pick = (
        expert_ids[:, :, None] == jnp.arange(experts, dtype=jnp.int32)[None, None, :]
    ).astype(jnp.float32)
    seed_expert = jnp.sum(expert_pick * (pair_grad * pick_group)[:, :, None], 1).reshape(
        tokens_here, groups, per_group
    )
    (grad_group, grad_expert), unused = lax.scan(
        partial(adjoint_step, targets), (seed_group, seed_expert), stored, reverse=True
    )
    d_group_logits = grad_group * group_aff * squashing(group_logits)
    d_expert_logits = (grad_expert * expert_aff).reshape(tokens_here, experts) * squashing(
        expert_logits
    )
    return (hidden_grad, d_group_logits, d_expert_logits)


def solution(mesh):
    in_specs = (
        P(("group", "expert"), None),
        P(("group", "expert"), None),
        P(("group", "expert"), None),
        P(("group", "expert"), None),
        P(("group", "expert"), None, None),
        P(("group", "expert"), None, None),
    )
    out_specs = (
        P(("group", "expert"), None, None),
        P(("group", "expert"), None),
        P(("group", "expert"), None),
    )
    return jax.shard_map(
        per_device, mesh=mesh, in_specs=in_specs, out_specs=out_specs, check_vma=False
    )
```

profile of v0, /device:TPU:0, one launch (start us, length us, event | category | flops | bytes accessed | tf_op | source)
XLA Modules:
  0.0 600.4 jit_solution(14312915412681843163)
XLA Ops:
  0.6 0.9 copy.101
  1.5 0.1 eq.55
  1.7 0.1 eq.51
  1.8 0.7 broadcast_multiply_fusion
  2.5 0.6 reduce-window.6
  3.1 0.2 slice_reduce_fusion
  3.4 0.1 mul.222
  3.7 1.4 scatter_custom_fusion.2
  5.2 1.4 scatter_custom_fusion.1
  6.8 4.2 gather_fusion
  10.9 3.6 fusion.16
  14.6 5.3 all-to-all-start.2
  20.1 0.1 reshape.221
  20.3 43.2 %all-to-all-done.2 = bf16[4,8,16,3584]{3,2,0,1:T(8,128)(2,1)} async-done(((bf16[4,8,16,3584]{3,2,0,1:T(8,128)(2,1)}), bf16[4,8,16,3584]{3,2,0,1:T(8,128)(2,1)}, u32[]{:S(2)}, u32[]{:S(2)}) %all-to-all-start.2) | async-done | bytes 3670048 | tf_op jit(solution)/shard_map/all_to_all | solution.py:64
  63.5 4.2 copy.114
  67.6 5.6 all-to-all-start.3
  73.2 264.1 %while.36 = (s32[]{:T(128)}, f32[128,4]{0,1:T(4,128)S(1)}, f32[128,4,8]{0,2,1:T(8,128)S(1)}, f32[5,128,4]{1,2,0:T(4,128)S(1)}, f32[5,128,4,8]{1,3,2,0:T(8,128)S(...) while((s32[]{:T(128)}, f32[128,4]{0,1:T(4,128)S(1)}, ...), condition=%wide.region_10.11_spmd, body=%wide.region_3.10_spmd.sunk | while | flops 15277 | bytes 133133 | solution.py:95
  73.4 100.2 %all-reduce.4 = (f32[4]{0:T(128)S(1)}, f32[4,8]{1,0:T(4,128)S(1)}) all-reduce(f32[4]{0:T(128)S(1)} %reduce_sum.212, f32[4,8]{1,0:T(4,128)S(1)} %reduce_sum.213), channel_id=1, replica_groups=mesh['group'=4,'expert'=8] {'group','expert'}, use_global_device_ids=true, to_apply=%region_5.5 | all-reduce | flops 36 | bytes 288 | tf_op jit(solution)/shard_map/while/body/eval_jaxpr/psum | solution.py:39
  173.9 0.3 fusion.45
  174.4 39.5 %all-reduce.4 = (f32[4]{0:T(128)S(1)}, f32[4,8]{1,0:T(4,128)S(1)}) all-reduce(f32[4]{0:T(128)S(1)} %reduce_sum.212, f32[4,8]{1,0:T(4,128)S(1)} %reduce_sum.213), channel_id=1, replica_groups=mesh['group'=4,'expert'=8] {'group','expert'}, use_global_device_ids=true, to_apply=%region_5.5 | all-reduce | flops 36 | bytes 288 | tf_op jit(solution)/shard_map/while/body/eval_jaxpr/psum | solution.py:39
  214.2 0.3 fusion.45
  214.7 40.5 %all-reduce.4 = (f32[4]{0:T(128)S(1)}, f32[4,8]{1,0:T(4,128)S(1)}) all-reduce(f32[4]{0:T(128)S(1)} %reduce_sum.212, f32[4,8]{1,0:T(4,128)S(1)} %reduce_sum.213), channel_id=1, replica_groups=mesh['group'=4,'expert'=8] {'group','expert'}, use_global_device_ids=true, to_apply=%region_5.5 | all-reduce | flops 36 | bytes 288 | tf_op jit(solution)/shard_map/while/body/eval_jaxpr/psum | solution.py:39
  255.4 0.3 fusion.45
  256.0 39.4 %all-reduce.4 = (f32[4]{0:T(128)S(1)}, f32[4,8]{1,0:T(4,128)S(1)}) all-reduce(f32[4]{0:T(128)S(1)} %reduce_sum.212, f32[4,8]{1,0:T(4,128)S(1)} %reduce_sum.213), channel_id=1, replica_groups=mesh['group'=4,'expert'=8] {'group','expert'}, use_global_device_ids=true, to_apply=%region_5.5 | all-reduce | flops 36 | bytes 288 | tf_op jit(solution)/shard_map/while/body/eval_jaxpr/psum | solution.py:39
  295.6 0.3 fusion.45
  296.1 40.6 %all-reduce.4 = (f32[4]{0:T(128)S(1)}, f32[4,8]{1,0:T(4,128)S(1)}) all-reduce(f32[4]{0:T(128)S(1)} %reduce_sum.212, f32[4,8]{1,0:T(4,128)S(1)} %reduce_sum.213), channel_id=1, replica_groups=mesh['group'=4,'expert'=8] {'group','expert'}, use_global_device_ids=true, to_apply=%region_5.5 | all-reduce | flops 36 | bytes 288 | tf_op jit(solution)/shard_map/while/body/eval_jaxpr/psum | solution.py:39
  336.9 0.3 fusion.45
  337.3 2.4 gather_fusion.2
  339.7 0.1 reshape.224
  340.0 0.1 reshape.227
  340.1 2.0 gather_fusion.3
  342.3 8.4 %fusion.17 = (f32[512]{0:T(512)S(1)}, f32[512,1024]{1,0:T(8,128)S(1)}) fusion(bf16[1,512,1024]{2,1,0:T(8,128)(2,1)} %param.14, bf16[512,3584]{1,0:T(8,128)(2,1)} %bitcast.18, bf16[1,1024,3584]{2,1,0:T(8,128)(2,1)} %param.15), kind=kOutput, calls=%fused_computation.49 | convolution fusion | flops 3759668736 | bytes 14157824 | tf_op jit(solution)/shard_map/dot_general | solution.py:126
  350.8 0.7 reshape.275
  351.5 3.4 all-to-all-start.4
  354.9 5.5 all-to-all-done.4
  360.4 0.5 broadcast.296
  360.9 0.7 reduce.2
  361.6 0.6 copy.115
  362.2 4.6 all-to-all-start.5
  366.9 4.7 all-to-all-done.5
  371.7 2.0 gather_fusion.1
  373.9 204.3 %while.37 = (s32[]{:T(128)}, f32[128,4]{0,1:T(4,128)S(1)}, f32[128,4,8]{0,2,1:T(8,128)S(1)}, f32[5,4]{1,0:T(8,128)S(1)}, f32[5,128,4]{1,2,0:T(4,128)S(1)}, /*ind...) while((s32[]{:T(128)}, f32[128,4]{0,1:T(4,128)S(1)}, ...), condition=%wide.region_28.29_spmd, body=%wide.region_19.28_spmd.sunk | while | flops 52050 | bytes 159945 | solution.py:157
  374.1 0.6 fusion.50
  375.0 38.3 %all-reduce.5 = (f32[4]{0:T(128)S(1)}, f32[4,8]{1,0:T(4,128)S(1)}) all-reduce(f32[4]{0:T(128)S(1)} %fusion.48, f32[4,8]{1,0:T(4,128)S(1)} %get-tuple-element.338), channel_id=1, replica_groups=mesh['group'=4,'expert'=8] {'group','expert'}, use_global_device_ids=true, to_apply=%region_23.23 | all-reduce | flops 36 | bytes 288 | tf_op jit(solution)/shard_map/while/body/eval_jaxpr/psum | solution.py:56
  413.5 0.6 fusion.50
  414.5 40.1 %all-reduce.5 = (f32[4]{0:T(128)S(1)}, f32[4,8]{1,0:T(4,128)S(1)}) all-reduce(f32[4]{0:T(128)S(1)} %fusion.48, f32[4,8]{1,0:T(4,128)S(1)} %get-tuple-element.338), channel_id=1, replica_groups=mesh['group'=4,'expert'=8] {'group','expert'}, use_global_device_ids=true, to_apply=%region_23.23 | all-reduce | flops 36 | bytes 288 | tf_op jit(solution)/shard_map/while/body/eval_jaxpr/psum | solution.py:56
  454.9 0.6 fusion.50
  455.8 39.9 %all-reduce.5 = (f32[4]{0:T(128)S(1)}, f32[4,8]{1,0:T(4,128)S(1)}) all-reduce(f32[4]{0:T(128)S(1)} %fusion.48, f32[4,8]{1,0:T(4,128)S(1)} %get-tuple-element.338), channel_id=1, replica_groups=mesh['group'=4,'expert'=8] {'group','expert'}, use_global_device_ids=true, to_apply=%region_23.23 | all-reduce | flops 36 | bytes 288 | tf_op jit(solution)/shard_map/while/body/eval_jaxpr/psum | solution.py:56
  496.0 0.6 fusion.50
  496.9 40.1 %all-reduce.5 = (f32[4]{0:T(128)S(1)}, f32[4,8]{1,0:T(4,128)S(1)}) all-reduce(f32[4]{0:T(128)S(1)} %fusion.48, f32[4,8]{1,0:T(4,128)S(1)} %get-tuple-element.338), channel_id=1, replica_groups=mesh['group'=4,'expert'=8] {'group','expert'}, use_global_device_ids=true, to_apply=%region_23.23 | all-reduce | flops 36 | bytes 288 | tf_op jit(solution)/shard_map/while/body/eval_jaxpr/psum | solution.py:56
  537.3 0.6 fusion.50
  538.3 39.8 %all-reduce.5 = (f32[4]{0:T(128)S(1)}, f32[4,8]{1,0:T(4,128)S(1)}) all-reduce(f32[4]{0:T(128)S(1)} %fusion.48, f32[4,8]{1,0:T(4,128)S(1)} %get-tuple-element.338), channel_id=1, replica_groups=mesh['group'=4,'expert'=8] {'group','expert'}, use_global_device_ids=true, to_apply=%region_23.23 | all-reduce | flops 36 | bytes 288 | tf_op jit(solution)/shard_map/while/body/eval_jaxpr/psum | solution.py:56
  578.3 0.1 copy.108
  578.4 0.2 reshape.237
  578.6 2.2 scatter_custom_fusion
  580.8 0.6 copy.109
  581.5 3.6 all-to-all-start
  585.0 0.6 bitcast_multiply_fusion.4
  585.6 4.1 all-to-all-done
  589.7 0.6 copy.110
  590.3 3.2 all-to-all-start.1
  593.6 0.6 subtract_multiply_fusion.2
  594.2 5.0 all-to-all-done.1
  599.2 1.2 fusion.18
  (156 shorter events, 6.7 us)
Async XLA Ops:
  0.6 6.1 %copy-start = (bf16[128,3584]{1,0:T(8,128)(2,1)S(1)}, bf16[128,3584]{1,0:T(8,128)(2,1)}, u32[]{:S(2)}) copy-start(bf16[128,3584]{1,0:T(8,128)(2,1)} %param.13) | copy-start | bytes 2752516
  14.6 5.4 copy-start.2
  14.6 5.7 copy-start.3
  14.6 5.7 copy-start.1
  14.6 48.9 %all-to-all-start.2 = ((bf16[4,8,16,3584]{3,2,0,1:T(8,128)(2,1)}), bf16[4,8,16,3584]{3,2,0,1:T(8,128)(2,1)}, u32[]{:S(2)}, u32[]{:S(2)}) async-start(bf16[4,8,16,3584]{3,2,0,1:T(8,128)(2,1)} %fusion.16), calls=%async_computation.2 | async-start | bytes 7340032 | tf_op jit(solution)/shard_map/all_to_all | solution.py:64
  67.6 274.7 %all-to-all-start.3 = ((bf16[4,8,16,3584]{3,2,1,0:T(8,128)(2,1)}), bf16[4,8,16,3584]{3,2,1,0:T(8,128)(2,1)}, u32[]{:S(2)}, u32[]{:S(2)}) async-start(bf16[4,8,16,3584]{3,2,1,0:T(8,128)(2,1)} %copy.114), calls=%async_computation.3 | async-start | bytes 7340032 | tf_op jit(solution)/shard_map/all_to_all | solution.py:68
  351.5 8.9 %all-to-all-start.4 = ((f32[4,1,128]{2,1,0:T(1,128)}), f32[4,1,128]{2,1,0:T(1,128)S(1)}, u32[]{:S(2)}, u32[]{:S(2)}) async-start(f32[4,1,128]{2,1,0:T(1,128)} %reshape.275), calls=%async_computation.4 | async-start | bytes 4096 | tf_op jit(solution)/shard_map/all_to_all | solution.py:133
  362.2 9.4 %all-to-all-start.5 = ((f32[4,8,16]{2,0,1:T(4,128)}), f32[4,8,16]{2,0,1:T(4,128)S(1)}, u32[]{:S(2)}, u32[]{:S(2)}) async-start(f32[4,8,16]{2,0,1:T(4,128)} %copy.115), calls=%async_computation.5 | async-start | bytes 32768 | tf_op jit(solution)/shard_map/all_to_all | solution.py:132
  581.5 8.3 %all-to-all-start = ((bf16[4,8,16]{2,0,1:T(4,128)(2,1)}), bf16[4,8,16]{2,0,1:T(4,128)(2,1)S(1)}, u32[]{:S(2)}, u32[]{:S(2)}) async-start(bf16[4,8,16]{2,0,1:T(4,128)(2,1)} %copy.109), calls=%async_computation | async-start | bytes 16384 | tf_op jit(solution)/shard_map/all_to_all | solution.py:65
  590.3 8.8 %all-to-all-start.1 = ((bf16[4,8,16]{2,1,0:T(8,128)(2,1)}), bf16[4,8,16]{2,1,0:T(8,128)(2,1)S(1)}, u32[]{:S(2)}, u32[]{:S(2)}) async-start(bf16[4,8,16]{2,1,0:T(8,128)(2,1)} %copy.110), calls=%async_computation.1 | async-start | bytes 16384 | tf_op jit(solution)/shard_map/all_to_all | solution.py:69
where the time goes:
time: 602 us; the launch traced here: 600 us
  blocking collectives  458 us (76%)
  waiting for transfers between devices  62.5 us (10%)
  local copies, waits for them, and re-layouts  26.5 us (4%)
  starting transfers between devices  25.7 us (4%)
  other arithmetic  17.9 us (3%)
  matrix products  8.44 us (1%)
    psum x5, blocking collectives, balance_step(): lax.psum((jnp.sum(group_in, 0), jnp.sum(expert_in, 0)), ('group', 'expert'))  260 us
    psum x5, blocking collectives, adjoint_step(): inner_g, inner_e = lax.psum((inner_g, inner_e), ('group', 'expert'))  198 us
    all_to_all x1, waiting for transfers between devices, deliver(): lax.all_to_all(payload[0], 'expert', split_axis=1, concat_axis=1, tiled=T...  43.2 us
  transfers between devices with their start and end apart: 6, of which 5 were waited for; matrix products, arithmetic and copies ran while one was open for 2% of the time, Pallas kernels for 0%

commit v1 on v0

--- a/solution.py
+++ b/solution.py
@@ -6,6 +6,18 @@
 
 ITERS = 5
 SOFTCAP = 4.0
+
+
+def serve_outputs(unit, ndim_at, m):
+    raw_out, clean = (unit.shape[:ndim_at], unit.shape[ndim_at + 1 :])
+    last = unit.reshape(*raw_out, m, -1, *clean)
+    return jnp.moveaxis(last, ndim_at, 0)
+
+
+def patch_fill(x0, join_dim):
+    outer = list(x0.shape[1:])
+    outer[join_dim] *= x0.shape[0]
+    return jnp.moveaxis(x0, 0, join_dim).reshape(outer)
 
 
 def capped(logits):
@@ -60,8 +72,25 @@
 
 
 def deliver(payload):
+
+    def create_ways(dev_axis, own_rows, packet, x_in):
+        p_next = jax.lax.axis_index(dev_axis)
+        known = jax.lax.axis_size(dev_axis)
+        y2, z = (known, p_next)
+        d_next = serve_outputs(packet, x_in, y2)
+        block_next = d_next
+        for to_i in range(1, y2):
+            item_now, passed = ((z + to_i) % y2, (z - to_i) % y2)
+            arr_out = lax.dynamic_index_in_dim(d_next, item_now, 0)
+            series = []
+            for k in range(y2):
+                series.append((k, (k + to_i) % y2))
+            n_now = jax.lax.ppermute(arr_out, dev_axis, series)
+            block_next = lax.dynamic_update_slice_in_dim(block_next, n_now, passed, axis=0)
+        return patch_fill(block_next, own_rows)
+
     halfway = (
-        lax.all_to_all(payload[0], "expert", split_axis=1, concat_axis=1, tiled=True),
+        create_ways("expert", 1, payload[0], 1),
         lax.all_to_all(payload[1], "expert", split_axis=1, concat_axis=1, tiled=True),
     )
     return (

time: 602 us -> 598 us (level)
  waiting for transfers between devices: 62.5 us -> 40 us
  starting transfers between devices: 25.7 us -> 36.7 us
    all_to_all x1 -> x0, waiting for transfers between devices: 43.2 us -> none  [deliver(): lax.all_to_all(payload[0], 'expert', split_axis=1, concat_axis=1, tiled=T...]
    ppermute x0 -> x7, waiting for transfers between devices: none -> 20.7 us  [create_ways(): n_now = jax.lax.ppermute(arr_out, dev_axis, series)]
    ppermute x0 -> x7, starting transfers between devices: none -> 17.2 us  [create_ways(): n_now = jax.lax.ppermute(arr_out, dev_axis, series)]
  transfers between devices with their start and end apart: 6 -> 12, of which waited for: 5 -> 7; matrix products, arithmetic and copies ran while one was open for 2% -> 3% of each run, Pallas kernels for 0% -> 0%
where the time goes in v1:
time: 598 us; the launch traced here: 596 us
  blocking collectives  461 us (77%)
  waiting for transfers between devices  40 us (7%)
  starting transfers between devices  36.7 us (6%)
  local copies, waits for them, and re-layouts  29.7 us (5%)
  other arithmetic  19.1 us (3%)
  matrix products  8.44 us (1%)
    psum x5, blocking collectives, balance_step(): lax.psum((jnp.sum(group_in, 0), jnp.sum(expert_in, 0)), ('group', 'expert'))  262 us
    psum x5, blocking collectives, adjoint_step(): inner_g, inner_e = lax.psum((inner_g, inner_e), ('group', 'expert'))  198 us
    ppermute x7, waiting for transfers between devices, create_ways(): n_now = jax.lax.ppermute(arr_out, dev_axis, series)  20.7 us
    ppermute x7, starting transfers between devices, create_ways(): n_now = jax.lax.ppermute(arr_out, dev_axis, series)  17.2 us
  transfers between devices with their start and end apart: 12, of which 7 were waited for; matrix products, arithmetic and copies ran while one was open for 3% of the time, Pallas kernels for 0%

profile of v1, /device:TPU:0, one launch (start us, length us, event | category | flops | bytes accessed | tf_op | source)
XLA Modules:
  0.0 595.9 jit_solution(8862308221108048610)
XLA Ops:
  0.6 0.9 copy.88
  1.8 0.7 broadcast_multiply_fusion
  2.5 0.6 reduce-window.6
  3.7 1.4 scatter_custom_fusion.1
  5.1 1.4 scatter_custom_fusion.2
  6.7 4.2 gather_fusion
  10.9 2.6 select_select_fusion
  13.4 1.7 dynamic-slice_bitcast_fusion
  15.7 2.5 collective-permute-start.1
  18.1 2.4 collective-permute-start.2
  20.6 0.5 collective-permute-start.3
  21.1 2.3 fusion.36
  24.0 5.1 collective-permute-done
  29.0 2.5 collective-permute-start.5
  31.5 0.8 constant_dynamic-update-slice_fusion.6
  32.4 8.7 %collective-permute-start.6 = (bf16[1,4,1,16,3584]{4,3,0,1,2:T(8,128)(2,1)}, bf16[1,4,1,16,3584]{4,3,0,1,2:T(8,128)(2,1)S(1)}, u32[]{:S(2)}, u32[]{:S(2)}) collective-permute-start(bf16[1,4,1,16,3584]{4,3,0,1,2:T(8,128)(2,1)} %get-tuple-element.239), channel_id=1, source_target_pairs={{0,7},{1,0},{2,1},{3,2},{4,3},{5,4},{6,5},{7,6},{8,15},{9,8},{10,9... | collective-permute-start | bytes 1376264 | tf_op jit(solution)/shard_map/ppermute | solution.py:88
  41.1 0.8 constant_dynamic-update-slice_fusion.5
  41.9 7.5 %collective-permute-done.2 = bf16[1,4,1,16,3584]{4,3,0,1,2:T(8,128)(2,1)S(1)} collective-permute-done((bf16[1,4,1,16,3584]{4,3,0,1,2:T(8,128)(2,1)}, bf16[1,4,1,16,3584]{4,3,0,1,2:T(8,128)(2,1)S(1)}, u32[]{:S(2)}, u32[]{:S(2)}) %collective-permute-start.2) | collective-permute-done | bytes 458784 | tf_op jit(solution)/shard_map/ppermute | solution.py:88
  49.4 0.8 constant_dynamic-update-slice_fusion.4
  50.2 0.8 constant_dynamic-update-slice_fusion.3
  51.0 8.2 %collective-permute-done.4 = bf16[1,4,1,16,3584]{4,3,0,1,2:T(8,128)(2,1)S(1)} collective-permute-done((bf16[1,4,1,16,3584]{4,3,0,1,2:T(8,128)(2,1)}, bf16[1,4,1,16,3584]{4,3,0,1,2:T(8,128)(2,1)S(1)}, u32[]{:S(2)}, u32[]{:S(2)}) %collective-permute-start.4) | collective-permute-done | bytes 458784 | tf_op jit(solution)/shard_map/ppermute | solution.py:88
  59.2 0.8 constant_dynamic-update-slice_fusion.2
  60.0 0.8 constant_dynamic-update-slice_fusion.1
  60.8 0.8 constant_dynamic-update-slice_fusion
  61.7 4.9 all-to-all-start.2
  66.5 266.4 %while.36 = (s32[]{:T(128)}, f32[128,4]{0,1:T(4,128)S(1)}, f32[128,4,8]{0,2,1:T(8,128)S(1)}, f32[5,128,4]{1,2,0:T(4,128)S(1)}, f32[5,128,4,8]{1,3,2,0:T(8,128)S(...) while((s32[]{:T(128)}, f32[128,4]{0,1:T(4,128)S(1)}, ...), condition=%wide.region_10.11_spmd, body=%wide.region_3.10_spmd.sunk | while | flops 15277 | bytes 133133 | solution.py:124
  66.8 102.8 %all-reduce.4 = (f32[4]{0:T(128)S(1)}, f32[4,8]{1,0:T(4,128)S(1)}) all-reduce(f32[4]{0:T(128)S(1)} %reduce_sum.212, f32[4,8]{1,0:T(4,128)S(1)} %reduce_sum.213), channel_id=1, replica_groups=mesh['group'=4,'expert'=8] {'group','expert'}, use_global_device_ids=true, to_apply=%region_5.5 | all-reduce | flops 36 | bytes 288 | tf_op jit(solution)/shard_map/while/body/eval_jaxpr/psum | solution.py:51
  170.3 39.1 %all-reduce.4 = (f32[4]{0:T(128)S(1)}, f32[4,8]{1,0:T(4,128)S(1)}) all-reduce(f32[4]{0:T(128)S(1)} %reduce_sum.212, f32[4,8]{1,0:T(4,128)S(1)} %reduce_sum.213), channel_id=1, replica_groups=mesh['group'=4,'expert'=8] {'group','expert'}, use_global_device_ids=true, to_apply=%region_5.5 | all-reduce | flops 36 | bytes 288 | tf_op jit(solution)/shard_map/while/body/eval_jaxpr/psum | solution.py:51
  210.3 40.7 %all-reduce.4 = (f32[4]{0:T(128)S(1)}, f32[4,8]{1,0:T(4,128)S(1)}) all-reduce(f32[4]{0:T(128)S(1)} %reduce_sum.212, f32[4,8]{1,0:T(4,128)S(1)} %reduce_sum.213), channel_id=1, replica_groups=mesh['group'=4,'expert'=8] {'group','expert'}, use_global_device_ids=true, to_apply=%region_5.5 | all-reduce | flops 36 | bytes 288 | tf_op jit(solution)/shard_map/while/body/eval_jaxpr/psum | solution.py:51
  251.8 39.1 %all-reduce.4 = (f32[4]{0:T(128)S(1)}, f32[4,8]{1,0:T(4,128)S(1)}) all-reduce(f32[4]{0:T(128)S(1)} %reduce_sum.212, f32[4,8]{1,0:T(4,128)S(1)} %reduce_sum.213), channel_id=1, replica_groups=mesh['group'=4,'expert'=8] {'group','expert'}, use_global_device_ids=true, to_apply=%region_5.5 | all-reduce | flops 36 | bytes 288 | tf_op jit(solution)/shard_map/while/body/eval_jaxpr/psum | solution.py:51
  291.6 40.7 %all-reduce.4 = (f32[4]{0:T(128)S(1)}, f32[4,8]{1,0:T(4,128)S(1)}) all-reduce(f32[4]{0:T(128)S(1)} %reduce_sum.212, f32[4,8]{1,0:T(4,128)S(1)} %reduce_sum.213), channel_id=1, replica_groups=mesh['group'=4,'expert'=8] {'group','expert'}, use_global_device_ids=true, to_apply=%region_5.5 | all-reduce | flops 36 | bytes 288 | tf_op jit(solution)/shard_map/while/body/eval_jaxpr/psum | solution.py:51
  332.9 2.4 gather_fusion.2
  335.8 2.0 gather_fusion.3
  338.0 8.4 %fusion.16 = (f32[512]{0:T(512)S(1)}, f32[512,1024]{1,0:T(8,128)S(1)}) fusion(bf16[1,512,1024]{2,1,0:T(8,128)(2,1)} %param.14, bf16[512,3584]{1,0:T(8,128)(2,1)} %bitcast.28, bf16[1,1024,3584]{2,1,0:T(8,128)(2,1)} %param.15), kind=kOutput, calls=%fused_computation.48 | convolution fusion | flops 3759668736 | bytes 14157824 | tf_op jit(solution)/shard_map/dot_general | solution.py:155
  346.5 0.7 reshape.301
  347.2 3.5 all-to-all-start.3
  350.8 5.5 all-to-all-done.3
  356.2 0.5 broadcast.336
  356.7 0.7 reduce.2
  357.5 0.6 copy.98
  358.1 4.3 all-to-all-start.4
  362.4 4.7 all-to-all-done.4
  367.2 1.9 gather_fusion.1
  369.5 204.3 %while.37 = (s32[]{:T(128)}, f32[128,4]{0,1:T(4,128)S(1)}, f32[128,4,8]{0,2,1:T(8,128)S(1)}, f32[5,4]{1,0:T(8,128)S(1)}, f32[5,128,4]{1,2,0:T(4,128)S(1)}, /*ind...) while((s32[]{:T(128)}, f32[128,4]{0,1:T(4,128)S(1)}, ...), condition=%wide.region_28.29_spmd, body=%wide.region_19.28_spmd.sunk | while | flops 52050 | bytes 159945 | solution.py:186
  369.6 0.6 fusion.50
  370.5 38.3 %all-reduce.5 = (f32[4]{0:T(128)S(1)}, f32[4,8]{1,0:T(4,128)S(1)}) all-reduce(f32[4]{0:T(128)S(1)} %fusion.48, f32[4,8]{1,0:T(4,128)S(1)} %get-tuple-element.346), channel_id=1, replica_groups=mesh['group'=4,'expert'=8] {'group','expert'}, use_global_device_ids=true, to_apply=%region_23.23 | all-reduce | flops 36 | bytes 288 | tf_op jit(solution)/shard_map/while/body/eval_jaxpr/psum | solution.py:68
  409.1 0.6 fusion.50
  410.0 40.1 %all-reduce.5 = (f32[4]{0:T(128)S(1)}, f32[4,8]{1,0:T(4,128)S(1)}) all-reduce(f32[4]{0:T(128)S(1)} %fusion.48, f32[4,8]{1,0:T(4,128)S(1)} %get-tuple-element.346), channel_id=1, replica_groups=mesh['group'=4,'expert'=8] {'group','expert'}, use_global_device_ids=true, to_apply=%region_23.23 | all-reduce | flops 36 | bytes 288 | tf_op jit(solution)/shard_map/while/body/eval_jaxpr/psum | solution.py:68
  450.4 0.6 fusion.50
  451.3 39.9 %all-reduce.5 = (f32[4]{0:T(128)S(1)}, f32[4,8]{1,0:T(4,128)S(1)}) all-reduce(f32[4]{0:T(128)S(1)} %fusion.48, f32[4,8]{1,0:T(4,128)S(1)} %get-tuple-element.346), channel_id=1, replica_groups=mesh['group'=4,'expert'=8] {'group','expert'}, use_global_device_ids=true, to_apply=%region_23.23 | all-reduce | flops 36 | bytes 288 | tf_op jit(solution)/shard_map/while/body/eval_jaxpr/psum | solution.py:68
  491.5 0.6 fusion.50
  492.4 40.1 %all-reduce.5 = (f32[4]{0:T(128)S(1)}, f32[4,8]{1,0:T(4,128)S(1)}) all-reduce(f32[4]{0:T(128)S(1)} %fusion.48, f32[4,8]{1,0:T(4,128)S(1)} %get-tuple-element.346), channel_id=1, replica_groups=mesh['group'=4,'expert'=8] {'group','expert'}, use_global_device_ids=true, to_apply=%region_23.23 | all-reduce | flops 36 | bytes 288 | tf_op jit(solution)/shard_map/while/body/eval_jaxpr/psum | solution.py:68
  532.8 0.6 fusion.50
  533.8 39.8 %all-reduce.5 = (f32[4]{0:T(128)S(1)}, f32[4,8]{1,0:T(4,128)S(1)}) all-reduce(f32[4]{0:T(128)S(1)} %fusion.48, f32[4,8]{1,0:T(4,128)S(1)} %get-tuple-element.346), channel_id=1, replica_groups=mesh['group'=4,'expert'=8] {'group','expert'}, use_global_device_ids=true, to_apply=%region_23.23 | all-reduce | flops 36 | bytes 288 | tf_op jit(solution)/shard_map/while/body/eval_jaxpr/psum | solution.py:68
  574.1 2.2 scatter_custom_fusion
  576.3 0.6 copy.96
  576.9 3.6 all-to-all-start
  580.5 0.6 bitcast_multiply_fusion.4
  581.1 4.1 all-to-all-done
  585.2 0.6 copy.97
  585.8 3.2 all-to-all-start.1
  589.1 0.6 subtract_multiply_fusion.2
  589.7 5.0 all-to-all-done.1
  594.7 1.2 fusion.17
  (175 shorter events, 10.3 us)
Async XLA Ops:
  0.6 6.1 %copy-start = (bf16[128,3584]{1,0:T(8,128)(2,1)S(1)}, bf16[128,3584]{1,0:T(8,128)(2,1)}, u32[]{:S(2)}) copy-start(bf16[128,3584]{1,0:T(8,128)(2,1)} %param.13) | copy-start | bytes 2752516
  13.4 7.7 %copy-start.1 = (bf16[512,3584]{1,0:T(8,128)(2,1)S(1)}, bf16[512,3584]{1,0:T(8,128)(2,1)}, u32[]{:S(2)}) copy-start(bf16[512,3584]{1,0:T(8,128)(2,1)} %gather_fusion) | copy-start | bytes 11010052
  15.2 13.9 %collective-permute-start = (bf16[1,4,1,16,3584]{4,3,0,1,2:T(8,128)(2,1)}, bf16[1,4,1,16,3584]{4,3,0,1,2:T(8,128)(2,1)S(1)}, u32[]{:S(2)}, u32[]{:S(2)}) collective-permute-start(bf16[1,4,1,16,3584]{4,3,0,1,2:T(8,128)(2,1)} %get-tuple-element.245), channel_id=1, source_target_pairs={{0,1},{1,2},{2,3},{3,4},{4,5},{5,6},{6,7},{7,0},{8,9},{9,10},{10,1... | collective-permute-start | bytes 1376264 | tf_op jit(solution)/shard_map/ppermute | solution.py:88
  15.7 16.7 %collective-permute-start.1 = (bf16[1,4,1,16,3584]{4,3,0,1,2:T(8,128)(2,1)}, bf16[1,4,1,16,3584]{4,3,0,1,2:T(8,128)(2,1)S(1)}, u32[]{:S(2)}, u32[]{:S(2)}) collective-permute-start(bf16[1,4,1,16,3584]{4,3,0,1,2:T(8,128)(2,1)} %get-tuple-element.244), channel_id=1, source_target_pairs={{0,2},{1,3},{2,4},{3,5},{4,6},{5,7},{6,0},{7,1},{8,10},{9,11},{10,... | collective-permute-start | bytes 1376264 | tf_op jit(solution)/shard_map/ppermute | solution.py:88
  18.1 31.2 %collective-permute-start.2 = (bf16[1,4,1,16,3584]{4,3,0,1,2:T(8,128)(2,1)}, bf16[1,4,1,16,3584]{4,3,0,1,2:T(8,128)(2,1)S(1)}, u32[]{:S(2)}, u32[]{:S(2)}) collective-permute-start(bf16[1,4,1,16,3584]{4,3,0,1,2:T(8,128)(2,1)} %get-tuple-element.243), channel_id=1, source_target_pairs={{0,3},{1,4},{2,5},{3,6},{4,7},{5,0},{6,1},{7,2},{8,11},{9,12},{10,... | collective-permute-start | bytes 1376264 | tf_op jit(solution)/shard_map/ppermute | solution.py:88
  20.6 29.6 %collective-permute-start.3 = (bf16[1,4,1,16,3584]{4,3,0,1,2:T(8,128)(2,1)}, bf16[1,4,1,16,3584]{4,3,0,1,2:T(8,128)(2,1)S(1)}, u32[]{:S(2)}, u32[]{:S(2)}) collective-permute-start(bf16[1,4,1,16,3584]{4,3,0,1,2:T(8,128)(2,1)} %get-tuple-element.242), channel_id=1, source_target_pairs={{0,4},{1,5},{2,6},{3,7},{4,0},{5,1},{6,2},{7,3},{8,12},{9,13},{10,... | collective-permute-start | bytes 1376264 | tf_op jit(solution)/shard_map/ppermute | solution.py:88
  21.1 2.4 copy-start.3
  21.1 2.9 copy-start.4
  21.1 2.9 copy-start.2
  21.1 38.1 %collective-permute-start.4 = (bf16[1,4,1,16,3584]{4,3,0,1,2:T(8,128)(2,1)}, bf16[1,4,1,16,3584]{4,3,0,1,2:T(8,128)(2,1)S(1)}, u32[]{:S(2)}, u32[]{:S(2)}) collective-permute-start(bf16[1,4,1,16,3584]{4,3,0,1,2:T(8,128)(2,1)} %get-tuple-element.241), channel_id=1, source_target_pairs={{0,5},{1,6},{2,7},{3,0},{4,1},{5,2},{6,3},{7,4},{8,13},{9,14},{10,... | collective-permute-start | bytes 1376264 | tf_op jit(solution)/shard_map/ppermute | solution.py:88
  29.0 31.0 %collective-permute-start.5 = (bf16[1,4,1,16,3584]{4,3,0,1,2:T(8,128)(2,1)}, bf16[1,4,1,16,3584]{4,3,0,1,2:T(8,128)(2,1)S(1)}, u32[]{:S(2)}, u32[]{:S(2)}) collective-permute-start(bf16[1,4,1,16,3584]{4,3,0,1,2:T(8,128)(2,1)} %get-tuple-element.240), channel_id=1, source_target_pairs={{0,6},{1,7},{2,0},{3,1},{4,2},{5,3},{6,4},{7,5},{8,14},{9,15},{10,... | collective-permute-start | bytes 1376264 | tf_op jit(solution)/shard_map/ppermute | solution.py:88
  32.4 28.5 %collective-permute-start.6 = (bf16[1,4,1,16,3584]{4,3,0,1,2:T(8,128)(2,1)}, bf16[1,4,1,16,3584]{4,3,0,1,2:T(8,128)(2,1)S(1)}, u32[]{:S(2)}, u32[]{:S(2)}) collective-permute-start(bf16[1,4,1,16,3584]{4,3,0,1,2:T(8,128)(2,1)} %get-tuple-element.239), channel_id=1, source_target_pairs={{0,7},{1,0},{2,1},{3,2},{4,3},{5,4},{6,5},{7,6},{8,15},{9,8},{10,9... | collective-permute-start | bytes 1376264 | tf_op jit(solution)/shard_map/ppermute | solution.py:88
  61.7 276.3 %all-to-all-start.2 = ((bf16[4,8,16,3584]{3,2,1,0:T(8,128)(2,1)}), bf16[4,8,16,3584]{3,2,1,0:T(8,128)(2,1)}, u32[]{:S(2)}, u32[]{:S(2)}) async-start(bf16[4,8,16,3584]{3,2,1,0:T(8,128)(2,1)} %bitcast.138), calls=%async_computation.2 | async-start | bytes 7340032 | tf_op jit(solution)/shard_map/all_to_all | solution.py:97
  347.2 9.0 %all-to-all-start.3 = ((f32[4,1,128]{2,1,0:T(1,128)}), f32[4,1,128]{2,1,0:T(1,128)S(1)}, u32[]{:S(2)}, u32[]{:S(2)}) async-start(f32[4,1,128]{2,1,0:T(1,128)} %reshape.301), calls=%async_computation.3 | async-start | bytes 4096 | tf_op jit(solution)/shard_map/all_to_all | solution.py:162
  358.1 9.0 %all-to-all-start.4 = ((f32[4,8,16]{2,0,1:T(4,128)}), f32[4,8,16]{2,0,1:T(4,128)S(1)}, u32[]{:S(2)}, u32[]{:S(2)}) async-start(f32[4,8,16]{2,0,1:T(4,128)} %copy.98), calls=%async_computation.4 | async-start | bytes 32768 | tf_op jit(solution)/shard_map/all_to_all | solution.py:161
  576.9 8.3 %all-to-all-start = ((bf16[4,8,16]{2,0,1:T(4,128)(2,1)}), bf16[4,8,16]{2,0,1:T(4,128)(2,1)S(1)}, u32[]{:S(2)}, u32[]{:S(2)}) async-start(bf16[4,8,16]{2,0,1:T(4,128)(2,1)} %copy.96), calls=%async_computation | async-start | bytes 16384 | tf_op jit(solution)/shard_map/all_to_all | solution.py:94
  585.8 8.8 %all-to-all-start.1 = ((bf16[4,8,16]{2,1,0:T(8,128)(2,1)}), bf16[4,8,16]{2,1,0:T(8,128)(2,1)S(1)}, u32[]{:S(2)}, u32[]{:S(2)}) async-start(bf16[4,8,16]{2,1,0:T(8,128)(2,1)} %copy.97), calls=%async_computation.1 | async-start | bytes 16384 | tf_op jit(solution)/shard_map/all_to_all | solution.py:98
